TPU v7x, 128 devices: a whole 4x4x4 slice. The times are simulated.
128 devices in a mesh: dp: 2 (over core), space: 64 (over y, z, x).
Axes of the slice: x: 4, y: 4, z: 4, core: 2. Of those that a mesh axis runs over, the one named last changes fastest.
Arguments:
- features: bfloat16 [2, 4096, 16, 1024], P('dp', 'space'), may hold values from -6 to 6
- psi: bfloat16 [2, 4096, 64, 256], P('dp', 'space'), may hold values from -0.75 to 0.75
- neighbors: int32 [2, 4096, 16], P('dp', 'space'), may hold values from 0 to 4095, as said below
- counts: int32 [2, 4096], P('dp', 'space'), may hold values from 4 to 16, as said below
- occupation: float32 [2, 256], P('dp'), may hold values from 0.1 to 1
- weights: bfloat16 [1024, 4096], P(None, 'space'), may hold values from -0.1875 to 0.1875
Outputs:
- energies: float32 [2, 256], P('dp')
- gradient: float32 [4096, 1024], P('space')
Inputs may be any that keep to these rules, and one draw needn't show every extreme that they name: `neighbors`: every neighbor tile lies in the same cluster of 64 consecutive tiles or in one of the two clusters beside it, counted around a closed loop of 64 clusters. `counts`: the first tile of every twist uses all 16 slots.
All inputs are finite; a program needn't handle non-finite values.
Results may differ from a plain program's by a relative error of at most 0.004.
Values may be sent and summed in bfloat16 or wider, within the bound.
No kernel may reach another device: no remote copies, remote signals or barrier semaphores. Data moves between devices by JAX's collectives and lax.ppermute only.
A program may use at most 192 MiB of HBM per device.

v0:
```python
import math
import jax
import jax.numpy as jnp
from jax import lax
from jax.sharding import PartitionSpec as P


def with_halo(value, sides, width):
    for axis, dim in sides:
        size, length = (lax.axis_size(axis), value.shape[dim])
        up = [(i, (i + 1) % size) for i in range(size)]
        down = [(j, i) for i, j in up]
        last = lax.slice_in_dim(value, length - width, length, axis=dim)
        leading = lax.slice_in_dim(value, 0, width, axis=dim)
        before = lax.ppermute(last, axis, up)
        after = lax.ppermute(leading, axis, down)
        value = jnp.concatenate([before, value, after], axis=dim)
    return value


def local(features, psi, neighbors, counts, occupation, weights):
    twists_here, rows, slots, width = features.shape
    orbit = psi.shape[2]
    bands = psi.shape[3]
    nspace = lax.axis_size("space")
    myself = lax.axis_index("space")
    factor = 1.0 / math.sqrt(rows * nspace * slots)
    flat = features.reshape(twists_here * rows * slots, width)
    products = jnp.dot(
        flat,
        lax.all_gather(weights, "space", axis=1, tiled=True),
        preferred_element_type=jnp.float32,
    )
    valid = (
        lax.broadcasted_iota(jnp.int32, (twists_here, rows, slots), 2) < counts[:, :, None]
    ).astype(jnp.bfloat16)
    blocks = (
        products.astype(jnp.bfloat16).reshape(twists_here, rows, slots, orbit, orbit)
        * valid[:, :, :, None, None]
    )
    widened = with_halo(psi, (("space", 1),), rows)
    owners = neighbors // rows
    placed = (owners - myself + 1 + nspace) % nspace * rows + neighbors % rows
    weighted = (psi.astype(jnp.float32) * occupation[:, None, None, :]).astype(jnp.bfloat16)

    def per_slot(carry, inputs):
        block_k, index_k, valid_k = inputs
        fetched = jax.vmap(lambda table, where: table[where])(widened, index_k)
        carry = carry + jnp.einsum(
            "trac,trcb->trab", block_k, fetched, preferred_element_type=jnp.float32
        )
        grad_k = (
            factor
            * jnp.einsum("trab,trcb->trac", weighted, fetched, preferred_element_type=jnp.float32)
        ).astype(jnp.bfloat16)
        return (carry, grad_k * valid_k[:, :, None, None])

    inputs = (jnp.moveaxis(blocks, 2, 0), jnp.moveaxis(placed, 2, 0), jnp.moveaxis(valid, 2, 0))
    applied, dblocks = lax.scan(
        per_slot, jnp.zeros((twists_here, rows, orbit, bands), jnp.float32), inputs
    )
    partial_energy = factor * jnp.sum(psi.astype(jnp.float32) * applied, axis=(1, 2))
    energies = lax.psum(partial_energy, "space")
    square = orbit * orbit
    flat_grads = dblocks.reshape(slots, twists_here, rows, square)
    share = lax.psum_scatter(
        jnp.einsum("strO,trsf->Of", flat_grads, features, preferred_element_type=jnp.float32),
        "space",
        scatter_dimension=0,
        tiled=True,
    )
    gradient = lax.psum(share, "dp")
    return (energies, gradient)


def solution(mesh):
    placed = (
        P("dp", "space", None, None),
        P("dp", "space", None, None),
        P("dp", "space", None),
        P("dp", "space"),
        P("dp", None),
        P(None, "space"),
    )
    return jax.shard_map(
        local,
        mesh=mesh,
        in_specs=placed,
        out_specs=(P("dp", None), P("space", None)),
        check_vma=False,
    )
```

profile of v0, /device:TPU:0, one launch (start us, length us, event | category | flops | bytes accessed | tf_op | source)
XLA Modules:
  0.0 1062.5 jit_solution(6959014675251214178)
XLA Ops:
  8.0 1.7 collective-permute-start
  9.6 7.3 collective-permute-start.1
  19.2 3.5 fusion.16
  22.7 41.5 %collective-permute-done = bf16[1,64,64,256]{3,2,1,0:T(8,128)(2,1)} collective-permute-done((bf16[1,64,64,256]{3,2,1,0:T(8,128)(2,1)}, bf16[1,64,64,256]{3,2,1,0:T(8,128)(2,1)}, u32[]{:S(2)}, u32[]{:S(2)}) %collective-permute-start) | collective-permute-done | bytes 2097184 | tf_op jit(solution)/shard_map/ppermute | solution.py:15
  64.2 5.5 pad_maximum_fusion
  69.7 51.4 %all-gather.2.cloned.1.call-done = bf16[1024,4096]{0,1:T(8,128)(2,1)} async-done(((bf16[1024,64]{0,1:T(8,128)(2,1)}), bf16[1024,4096]{0,1:T(8,128)(2,1)}) %all-gather.2.cloned.1.call-update) | async-done | bytes 8388624 | tf_op jit(solution)/shard_map/all_gather | solution.py:31
  121.1 14.3 %convolution_convert_fusion = bf16[1024,4096]{1,0:T(8,128)(2,1)} fusion(bf16[1024,1024]{1,0:T(8,128)(2,1)S(1)} %bitcast.74, bf16[1024,4096]{0,1:T(8,128)(2,1)} %all-gather.2.cloned.1.call-done), kind=kOutput, calls=%fused_computation.21 | convolution fusion | flops 8594128896 | bytes 18874368 | tf_op jit(solution)/shard_map/dot_general | solution.py:29
  135.4 23.6 %reshape.163 = bf16[1,64,16,64,64]{4,3,2,1,0:T(8,128)(2,1)} reshape(bf16[1024,4096]{1,0:T(8,128)(2,1)} %convolution_convert_fusion) | data formatting | bytes 16777216 | tf_op jit(solution)/shard_map/reshape | solution.py:38
  159.0 14.0 %fusion.15 = bf16[16,1,64,64,64]{4,3,2,1,0:T(8,128)(2,1)} fusion(bf16[1,64,16,64,64]{4,3,2,1,0:T(8,128)(2,1)} %reshape.163, bf16[64,16]{0,1:T(8,128)(2,1)S(1)} %fusion.24), kind=kLoop, calls=%fused_computation.19 | loop fusion | flops 4194304 | bytes 16779264 | tf_op jit(solution)/shard_map/transpose | solution.py:58
  173.0 274.1 %while.13 = (s32[]{:T(128)}, f32[1,64,64,256]{3,2,1,0:T(8,128)}, bf16[16,1,64,64,64]{4,3,2,0,1:T(8,128)(2,1)}, bf16[16,1,64,64,64]{4,3,2,1,0:T(8,128)(2,1)}, s32...) while((s32[]{:T(128)}, f32[1,64,64,256]{3,2,1,0:T(8,128)}, ...), condition=%wide.region_1.2_spmd.clone, body=%wide.region_0.1_spmd.clone.sunk | while | flops 271319552 | bytes 23071752 | solution.py:59
  173.0 4.8 gather_fusion
  177.8 3.9 fusion.41
  183.3 4.6 bitcast_add_fusion.2
  189.0 4.8 gather_fusion
  193.8 3.9 fusion.41
  199.3 5.8 bitcast_add_fusion.2
  206.2 4.8 gather_fusion
  211.0 3.9 fusion.41
  216.5 5.8 bitcast_add_fusion.2
  223.5 4.8 gather_fusion
  228.2 3.9 fusion.41
  233.7 5.8 bitcast_add_fusion.2
  240.6 4.8 gather_fusion
  245.4 3.9 fusion.41
  250.9 5.8 bitcast_add_fusion.2
  257.8 4.8 gather_fusion
  262.6 3.9 fusion.41
  268.1 5.8 bitcast_add_fusion.2
  275.0 4.8 gather_fusion
  279.8 3.9 fusion.41
  285.3 5.8 bitcast_add_fusion.2
  292.3 4.8 gather_fusion
  297.0 3.9 fusion.41
  302.5 5.8 bitcast_add_fusion.2
  309.5 4.8 gather_fusion
  314.2 3.9 fusion.41
  319.7 5.8 bitcast_add_fusion.2
  326.7 4.8 gather_fusion
  331.5 3.9 fusion.41
  337.0 5.8 bitcast_add_fusion.2
  343.9 4.8 gather_fusion
  348.7 3.9 fusion.41
  354.2 5.8 bitcast_add_fusion.2
  361.1 4.8 gather_fusion
  365.8 3.9 fusion.41
  371.4 5.8 bitcast_add_fusion.2
  378.3 4.8 gather_fusion
  383.0 3.9 fusion.41
  388.5 5.8 bitcast_add_fusion.2
  395.5 4.8 gather_fusion
  400.3 3.9 fusion.41
  405.8 5.8 bitcast_add_fusion.2
  412.7 4.8 gather_fusion
  417.5 3.9 fusion.41
  423.0 5.8 bitcast_add_fusion.2
  429.9 4.8 gather_fusion
  434.7 3.9 fusion.41
  440.2 5.8 bitcast_add_fusion.2
  447.1 22.6 %reshape.164 = bf16[16,64,4096]{2,1,0:T(8,128)(2,1)} reshape(bf16[16,1,64,64,64]{4,3,2,0,1:T(8,128)(2,1)} %get-tuple-element.46) | data formatting | bytes 16777216 | tf_op jit(solution)/shard_map/reshape.16
  469.7 15.7 %convolution_bitcast_fusion = f32[4096,1024]{1,0:T(8,128)} fusion(bf16[16,64,4096]{2,1,0:T(8,128)(2,1)} %reshape.164, bf16[64,16,1024]{2,1,0:T(8,128)(2,1)S(1)} %bitcast.75), kind=kOutput, calls=%fused_computation.20 | convolution fusion | flops 8589934592 | bytes 27262976 | tf_op jit(solution)/shard_map/strO,trsf->Of/dot_general | solution.py:67
  485.4 392.0 %reduce-scatter.2.cloned.1.call-done = f32[64,1024]{1,0:T(8,128)} async-done(((f32[4096,1024]{1,0:T(8,128)}), f32[64,1024]{1,0:T(8,128)}) %reduce-scatter.2.cloned.1.call-update) | async-done | bytes 262160 | tf_op jit(solution)/shard_map/reduce_scatter | solution.py:66
  877.4 3.5 fusion.17
  880.9 173.4 %psum.14 = f32[1,256]{1,0:T(1,128)} all-reduce(f32[1,256]{1,0:T(1,128)S(1)} %bitcast.77), channel_id=1, replica_groups=mesh['dp'=2,'space'=64] {'space'}, use_global_device_ids=true, to_apply=%region_3.4 | all-reduce | flops 256 | bytes 2048 | tf_op jit(solution)/shard_map/psum | solution.py:63
  1054.3 1.7 copy.41
  (114 shorter events, 46.2 us)
Async XLA Ops:
  7.2 114.0 %copy-start = (bf16[1,64,16,1024]{3,2,1,0:T(8,128)(2,1)S(1)}, bf16[1,64,16,1024]{3,2,1,0:T(8,128)(2,1)}, u32[]{:S(2)}) copy-start(bf16[1,64,16,1024]{3,2,1,0:T(8,128)(2,1)} %param.8) | copy-start | bytes 6291460
  7.2 113.9 %all-gather.2.cloned.1.call-start = ((), (), s32[]{:S(2)}) async-start(), calls=%async_computation.1 | async-start | bytes 8519680 | tf_op jit(solution)/shard_map/all_gather | solution.py:31
  7.9 869.5 %reduce-scatter.2.cloned.1.call-start = ((), (), s32[]{:S(2)}) async-start(), calls=%async_computation.2 | async-start | bytes 17039360 | tf_op jit(solution)/shard_map/reduce_scatter | solution.py:66
  8.0 56.2 %collective-permute-start = (bf16[1,64,64,256]{3,2,1,0:T(8,128)(2,1)}, bf16[1,64,64,256]{3,2,1,0:T(8,128)(2,1)}, u32[]{:S(2)}, u32[]{:S(2)}) collective-permute-start(bf16[1,64,64,256]{3,2,1,0:T(8,128)(2,1)} %param.9), channel_id=1, source_target_pairs={{0,1},{1,2},{2,3},{3,4},{4,5},{5,6},{6,7},{7,8},{8,9},{9,10},{10,1... | collective-permute-start | bytes 6291464 | tf_op jit(solution)/shard_map/ppermute | solution.py:15
  9.6 54.6 %collective-permute-start.1 = (bf16[1,64,64,256]{3,2,1,0:T(8,128)(2,1)}, bf16[1,64,64,256]{3,2,1,0:T(8,128)(2,1)}, u32[]{:S(2)}, u32[]{:S(2)}) collective-permute-start(bf16[1,64,64,256]{3,2,1,0:T(8,128)(2,1)} %param.9), channel_id=1, source_target_pairs={{1,0},{2,1},{3,2},{4,3},{5,4},{6,5},{7,6},{8,7},{9,8},{10,9},{11,1... | collective-permute-start | bytes 6291464 | tf_op jit(solution)/shard_map/ppermute | solution.py:16
  16.9 47.3 %copy-start.1 = (bf16[1,64,64,256]{3,2,1,0:T(8,128)(2,1)S(1)}, bf16[1,64,64,256]{3,2,1,0:T(8,128)(2,1)}, u32[]{:S(2)}) copy-start(bf16[1,64,64,256]{3,2,1,0:T(8,128)(2,1)} %param.9) | copy-start | bytes 6291460
  485.4 568.9 %all-reduce.2.cloned.1.call-start = ((), (), s32[]{:S(2)}) async-start(), calls=%async_computation.3 | async-start | bytes 524288 | tf_op jit(solution)/shard_map/psum | solution.py:72
Sparse Core Ops, SparseCore 0:
  10.9 110.2 all-gather.1
  485.5 391.8 reduce-scatter.1
  879.8 18.4 all-reduce.1
where the time goes:
time: 1070 us; the launch traced here: 1060 us
  waiting for transfers between devices  486 us (45%)
  matrix products  184 us (17%)
  blocking collectives  173 us (16%)
  local copies, waits for them, and re-layouts  167 us (16%)
  other arithmetic  28.9 us (3%)
  between operations  13.8 us (1%)
    reduce_scatter x1, waiting for transfers between devices, local(): lax.psum_scatter(jnp.einsum('strO,trsf->Of', flat_grads, features, prefer...  392 us
    psum x1, blocking collectives, local(): energies = lax.psum(partial_energy, 'space')  173 us
    dot_general x16, matrix products, per_slot(): jnp.einsum('trac,trcb->trab', block_k, fetched, preferred_element_type=jn...  92 us
    gather x32, local copies, waits for them, and re-layouts, per_slot(): fetched = jax.vmap(lambda table, where: table[where])(widened, index_k)  76.5 us
    dot_general x16, matrix products, per_slot(): jnp.einsum('trab,trcb->trac', weighted, fetched, preferred_element_type=j...  62.4 us
    all_gather x1, waiting for transfers between devices, local(): lax.all_gather(weights, 'space', axis=1, tiled=True)  51.4 us
    dynamic_update_slice x32, local copies, waits for them, and re-layouts, local(): lax.scan(per_slot, jnp.zeros((twists_here, rows, orbit, bands), jnp.float...  42.7 us
    ppermute x1, waiting for transfers between devices, with_halo(): before = lax.ppermute(last, axis, up)  41.5 us
  transfers between devices with their start and end apart: 5, of which 3 were waited for; matrix products, arithmetic and copies ran while one was open for 1% of the time, Pallas kernels for 0%

commit v1 on v0

--- a/solution.py
+++ b/solution.py
@@ -60,7 +60,7 @@
         per_slot, jnp.zeros((twists_here, rows, orbit, bands), jnp.float32), inputs
     )
     partial_energy = factor * jnp.sum(psi.astype(jnp.float32) * applied, axis=(1, 2))
-    energies = lax.psum(partial_energy, "space")
+    energies = jnp.sum(lax.all_gather(partial_energy, "space"), axis=0)
     square = orbit * orbit
     flat_grads = dblocks.reshape(slots, twists_here, rows, square)
     share = lax.psum_scatter(

time: 1070 us -> 1060 us (level)
    psum x1 -> x0, blocking collectives: 173 us -> none  [local(): energies = lax.psum(partial_energy, 'space')]
    all_gather x0 -> x1, blocking collectives: none -> 171 us  [local(): energies = jnp.sum(lax.all_gather(partial_energy, 'space'), axis=0)]
where the time goes in v1:
time: 1060 us
  waiting for transfers between devices  486 us (46%)
  matrix products  184 us (17%)
  blocking collectives  171 us (16%)
  local copies, waits for them, and re-layouts  167 us (16%)
  other arithmetic  29.6 us (3%)
  between operations  13.8 us (1%)
    reduce_scatter x1, waiting for transfers between devices, local(): lax.psum_scatter(jnp.einsum('strO,trsf->Of', flat_grads, features, prefer...  392 us
    all_gather x1, blocking collectives, local(): energies = jnp.sum(lax.all_gather(partial_energy, 'space'), axis=0)  171 us
    dot_general x16, matrix products, per_slot(): jnp.einsum('trac,trcb->trab', block_k, fetched, preferred_element_type=jn...  92 us
    gather x32, local copies, waits for them, and re-layouts, per_slot(): fetched = jax.vmap(lambda table, where: table[where])(widened, index_k)  76.5 us
    dot_general x16, matrix products, per_slot(): jnp.einsum('trab,trcb->trac', weighted, fetched, preferred_element_type=j...  62.4 us
    all_gather x1, waiting for transfers between devices, local(): lax.all_gather(weights, 'space', axis=1, tiled=True)  51.4 us
    dynamic_update_slice x32, local copies, waits for them, and re-layouts, local(): lax.scan(per_slot, jnp.zeros((twists_here, rows, orbit, bands), jnp.float...  42.7 us
    ppermute x1, waiting for transfers between devices, with_halo(): before = lax.ppermute(last, axis, up)  41.5 us
  transfers between devices with their start and end apart: 5, of which 3 were waited for; matrix products, arithmetic and copies ran while one was open for 1% of the time, Pallas kernels for 0%

profile of v1, /device:TPU:0, one launch (start us, length us, event | category | flops | bytes accessed | tf_op | source)
XLA Modules:
  0.0 1060.3 jit_solution(6451055596835501936)
XLA Ops:
  8.0 1.7 collective-permute-start
  9.6 7.3 collective-permute-start.1
  19.2 3.5 fusion.16
  22.7 41.5 %collective-permute-done = bf16[1,64,64,256]{3,2,1,0:T(8,128)(2,1)} collective-permute-done((bf16[1,64,64,256]{3,2,1,0:T(8,128)(2,1)}, bf16[1,64,64,256]{3,2,1,0:T(8,128)(2,1)}, u32[]{:S(2)}, u32[]{:S(2)}) %collective-permute-start) | collective-permute-done | bytes 2097184 | tf_op jit(solution)/shard_map/ppermute | solution.py:15
  64.2 5.5 pad_maximum_fusion
  69.7 51.4 %all-gather.4.cloned.1.call-done = bf16[1024,4096]{0,1:T(8,128)(2,1)} async-done(((bf16[1024,64]{0,1:T(8,128)(2,1)}), bf16[1024,4096]{0,1:T(8,128)(2,1)}) %all-gather.4.cloned.1.call-update) | async-done | bytes 8388624 | tf_op jit(solution)/shard_map/all_gather | solution.py:31
  121.1 14.3 %convolution_convert_fusion = bf16[1024,4096]{1,0:T(8,128)(2,1)} fusion(bf16[1024,1024]{1,0:T(8,128)(2,1)S(1)} %bitcast.75, bf16[1024,4096]{0,1:T(8,128)(2,1)} %all-gather.4.cloned.1.call-done), kind=kOutput, calls=%fused_computation.21 | convolution fusion | flops 8594128896 | bytes 18874368 | tf_op jit(solution)/shard_map/dot_general | solution.py:29
  135.4 23.6 %reshape.166 = bf16[1,64,16,64,64]{4,3,2,1,0:T(8,128)(2,1)} reshape(bf16[1024,4096]{1,0:T(8,128)(2,1)} %convolution_convert_fusion) | data formatting | bytes 16777216 | tf_op jit(solution)/shard_map/reshape | solution.py:38
  159.0 14.0 %fusion.15 = bf16[16,1,64,64,64]{4,3,2,1,0:T(8,128)(2,1)} fusion(bf16[1,64,16,64,64]{4,3,2,1,0:T(8,128)(2,1)} %reshape.166, bf16[64,16]{0,1:T(8,128)(2,1)S(1)} %fusion.24), kind=kLoop, calls=%fused_computation.19 | loop fusion | flops 4194304 | bytes 16779264 | tf_op jit(solution)/shard_map/transpose | solution.py:58
  173.0 274.1 %while.13 = (s32[]{:T(128)}, f32[1,64,64,256]{3,2,1,0:T(8,128)}, bf16[16,1,64,64,64]{4,3,2,0,1:T(8,128)(2,1)}, bf16[16,1,64,64,64]{4,3,2,1,0:T(8,128)(2,1)}, s32...) while((s32[]{:T(128)}, f32[1,64,64,256]{3,2,1,0:T(8,128)}, ...), condition=%wide.region_1.2_spmd.clone, body=%wide.region_0.1_spmd.clone.sunk | while | flops 271319552 | bytes 23071752 | solution.py:59
  173.0 4.8 gather_fusion
  177.8 3.9 fusion.41
  183.3 4.6 bitcast_add_fusion.2
  189.0 4.8 gather_fusion
  193.8 3.9 fusion.41
  199.3 5.8 bitcast_add_fusion.2
  206.2 4.8 gather_fusion
  211.0 3.9 fusion.41
  216.5 5.8 bitcast_add_fusion.2
  223.5 4.8 gather_fusion
  228.2 3.9 fusion.41
  233.7 5.8 bitcast_add_fusion.2
  240.6 4.8 gather_fusion
  245.4 3.9 fusion.41
  250.9 5.8 bitcast_add_fusion.2
  257.8 4.8 gather_fusion
  262.6 3.9 fusion.41
  268.1 5.8 bitcast_add_fusion.2
  275.0 4.8 gather_fusion
  279.8 3.9 fusion.41
  285.3 5.8 bitcast_add_fusion.2
  292.3 4.8 gather_fusion
  297.0 3.9 fusion.41
  302.5 5.8 bitcast_add_fusion.2
  309.5 4.8 gather_fusion
  314.2 3.9 fusion.41
  319.7 5.8 bitcast_add_fusion.2
  326.7 4.8 gather_fusion
  331.5 3.9 fusion.41
  337.0 5.8 bitcast_add_fusion.2
  343.9 4.8 gather_fusion
  348.7 3.9 fusion.41
  354.2 5.8 bitcast_add_fusion.2
  361.1 4.8 gather_fusion
  365.8 3.9 fusion.41
  371.4 5.8 bitcast_add_fusion.2
  378.3 4.8 gather_fusion
  383.0 3.9 fusion.41
  388.5 5.8 bitcast_add_fusion.2
  395.5 4.8 gather_fusion
  400.3 3.9 fusion.41
  405.8 5.8 bitcast_add_fusion.2
  412.7 4.8 gather_fusion
  417.5 3.9 fusion.41
  423.0 5.8 bitcast_add_fusion.2
  429.9 4.8 gather_fusion
  434.7 3.9 fusion.41
  440.2 5.8 bitcast_add_fusion.2
  447.1 22.6 %reshape.167 = bf16[16,64,4096]{2,1,0:T(8,128)(2,1)} reshape(bf16[16,1,64,64,64]{4,3,2,0,1:T(8,128)(2,1)} %get-tuple-element.46) | data formatting | bytes 16777216 | tf_op jit(solution)/shard_map/reshape.16
  469.7 15.7 %convolution_bitcast_fusion = f32[4096,1024]{1,0:T(8,128)} fusion(bf16[16,64,4096]{2,1,0:T(8,128)(2,1)} %reshape.167, bf16[64,16,1024]{2,1,0:T(8,128)(2,1)S(1)} %bitcast.76), kind=kOutput, calls=%fused_computation.20 | convolution fusion | flops 8589934592 | bytes 27262976 | tf_op jit(solution)/shard_map/strO,trsf->Of/dot_general | solution.py:67
  485.4 392.0 %reduce-scatter.2.cloned.1.call-done = f32[64,1024]{1,0:T(8,128)} async-done(((f32[4096,1024]{1,0:T(8,128)}), f32[64,1024]{1,0:T(8,128)}) %reduce-scatter.2.cloned.1.call-update) | async-done | bytes 262160 | tf_op jit(solution)/shard_map/reduce_scatter | solution.py:66
  877.4 3.5 fusion.17
  880.9 170.6 %all-gather.1 = f32[64,1,256]{2,1,0:T(1,128)S(1)} all-gather(f32[1,1,256]{2,1,0:T(1,128)S(1)} %bitcast.78), channel_id=2, replica_groups=mesh['dp'=2,'space'=64] {'space'}, dimensions={0}, use_global_device_ids=true | all-gather | bytes 66560 | tf_op jit(solution)/shard_map/all_gather | solution.py:63
  1052.1 1.7 copy.48
  (115 shorter events, 46.9 us)
Async XLA Ops:
  7.2 114.0 %copy-start = (bf16[1,64,16,1024]{3,2,1,0:T(8,128)(2,1)S(1)}, bf16[1,64,16,1024]{3,2,1,0:T(8,128)(2,1)}, u32[]{:S(2)}) copy-start(bf16[1,64,16,1024]{3,2,1,0:T(8,128)(2,1)} %param.8) | copy-start | bytes 6291460
  7.2 113.9 %all-gather.4.cloned.1.call-start = ((), (), s32[]{:S(2)}) async-start(), calls=%async_computation.1 | async-start | bytes 8519680 | tf_op jit(solution)/shard_map/all_gather | solution.py:31
  7.9 869.5 %reduce-scatter.2.cloned.1.call-start = ((), (), s32[]{:S(2)}) async-start(), calls=%async_computation.2 | async-start | bytes 17039360 | tf_op jit(solution)/shard_map/reduce_scatter | solution.py:66
  8.0 56.2 %collective-permute-start = (bf16[1,64,64,256]{3,2,1,0:T(8,128)(2,1)}, bf16[1,64,64,256]{3,2,1,0:T(8,128)(2,1)}, u32[]{:S(2)}, u32[]{:S(2)}) collective-permute-start(bf16[1,64,64,256]{3,2,1,0:T(8,128)(2,1)} %param.9), channel_id=1, source_target_pairs={{0,1},{1,2},{2,3},{3,4},{4,5},{5,6},{6,7},{7,8},{8,9},{9,10},{10,1... | collective-permute-start | bytes 6291464 | tf_op jit(solution)/shard_map/ppermute | solution.py:15
  9.6 54.6 %collective-permute-start.1 = (bf16[1,64,64,256]{3,2,1,0:T(8,128)(2,1)}, bf16[1,64,64,256]{3,2,1,0:T(8,128)(2,1)}, u32[]{:S(2)}, u32[]{:S(2)}) collective-permute-start(bf16[1,64,64,256]{3,2,1,0:T(8,128)(2,1)} %param.9), channel_id=1, source_target_pairs={{1,0},{2,1},{3,2},{4,3},{5,4},{6,5},{7,6},{8,7},{9,8},{10,9},{11,1... | collective-permute-start | bytes 6291464 | tf_op jit(solution)/shard_map/ppermute | solution.py:16
  16.9 47.3 %copy-start.1 = (bf16[1,64,64,256]{3,2,1,0:T(8,128)(2,1)S(1)}, bf16[1,64,64,256]{3,2,1,0:T(8,128)(2,1)}, u32[]{:S(2)}) copy-start(bf16[1,64,64,256]{3,2,1,0:T(8,128)(2,1)} %param.9) | copy-start | bytes 6291460
  485.4 566.8 %all-reduce.2.cloned.1.call-start = ((), (), s32[]{:S(2)}) async-start(), calls=%async_computation.3 | async-start | bytes 524288 | tf_op jit(solution)/shard_map/psum | solution.py:72
Sparse Core Ops, SparseCore 0:
  10.9 110.2 all-gather.3
  485.5 391.8 reduce-scatter.1
  879.8 18.4 all-reduce.1
